TPU v7x, 32 devices: a whole 2x2x4 slice. The times are simulated.
32 devices in a mesh: py: 4 (over y, x), pz: 8 (over z, core).
Axes of the slice: x: 2, y: 2, z: 4, core: 2. Of those that a mesh axis runs over, the one named last changes fastest.
Arguments:
- field_one: float32 [256, 256, 512], P('py', 'pz'), may hold values from -6 to 6
- field_two: float32 [256, 256, 512], P('py', 'pz'), may hold values from -6 to 6
- coef: float32 [2, 2, 8], replicated, may hold values from -4 to 4
Outputs:
- potential_one: float32 [256, 256, 512], P('py', 'pz')
- potential_two: float32 [256, 256, 512], P('py', 'pz')
All inputs are finite; a program needn't handle non-finite values.
Results may differ from a plain program's by a relative error of at most 0.00013.
Values sent between devices are 32-bit elements; how exact they have to be, the bound alone decides.
No kernel may reach another device: no remote copies, remote signals or barrier semaphores. Data moves between devices by JAX's collectives and lax.ppermute only.
A program may use at most 256 MiB of HBM per device.

v0:
```python
import math
import jax
import jax.numpy as jnp
from jax import lax
from jax.sharding import PartitionSpec as P

HIGH = lax.Precision.HIGHEST


def padded_2(value, sides, width):
    for axis, dim in sides:
        size, length = (lax.axis_size(axis), value.shape[dim])
        up = [(i, (i + 1) % size) for i in range(size)]
        down = [(j, i) for i, j in up]
        last = lax.slice_in_dim(value, length - width, length, axis=dim)
        leading = lax.slice_in_dim(value, 0, width, axis=dim)
        before = lax.ppermute(last, axis, up)
        after = lax.ppermute(leading, axis, down)
        value = jnp.concatenate([before, value, after], axis=dim)
    return value


def freq_at(position, length):
    paired = position // 2
    odd_bit = position % 2
    inner = jnp.where(odd_bit == 0, paired, length - paired)
    return jnp.where(paired == 0, odd_bit * (length // 2), inner)


def scaled_signed(freq, length):
    return jnp.where(freq > length // 2, freq - length, freq).astype(jnp.float32) / length


def forward_table(length):
    indices = jnp.arange(length, dtype=jnp.int32)
    freq = freq_at(indices, length)
    phase = indices[:, None] * freq[None, :] % length
    angle = 2.0 * math.pi / length * phase.astype(jnp.float32)
    return (jnp.cos(angle), jnp.sin(angle))


def inverse_table(length):
    cosine, sine = forward_table(length)
    return (cosine.T / length, sine.T / length)


def contract(form, data, table):
    return jnp.einsum(form, data, table, precision=HIGH)


def complex_apply(form, real_part, imag_part, cosine, sine, sign):
    if imag_part is None:
        return (contract(form, real_part, cosine), -sign * contract(form, real_part, sine))
    real_out = contract(form, real_part, cosine) + sign * contract(form, imag_part, sine)
    imag_out = contract(form, imag_part, cosine) - sign * contract(form, real_part, sine)
    return (real_out, imag_out)


def make_kernel(coef, freqs, lengths):
    radius = scaled_signed(freqs[0], lengths[0]) ** 2 + scaled_signed(freqs[1], lengths[1]) ** 2
    radius = radius + scaled_signed(freqs[2], lengths[2]) ** 2
    ratio = 4.0 * radius / 3.0
    volume = ratio * jnp.sqrt(ratio)
    basis_count = coef.shape[2]
    centres = (jnp.arange(basis_count, dtype=jnp.float32) + 0.5) / basis_count
    basis = jnp.exp(-jnp.square((volume[None] - centres[:, None, None, None]) * basis_count))
    kernel = jnp.einsum("abr,rkxm->abkxm", coef, basis, precision=HIGH)
    return kernel


def shards(field_one, field_two, coef):
    y_local, z_local, x_count = field_one.shape
    py_count = lax.axis_size("py")
    pz_count = lax.axis_size("pz")
    y_count = y_local * py_count
    z_count = z_local * pz_count
    x_block = x_count // py_count
    ky_block = y_count // pz_count
    cells = y_local * z_local
    fields = jnp.stack([field_one, field_two])
    along_x = (4.0 * fields + jnp.roll(fields, 1, 3) + jnp.roll(fields, -1, 3)) / 6.0
    padded = padded_2(along_x, (("py", 1), ("pz", 2)), 1)
    along_y = (4.0 * padded[:, 1:-1] + padded[:, 2:] + padded[:, :-2]) / 6.0
    smoothed = (4.0 * along_y[:, :, 1:-1] + along_y[:, :, 2:] + along_y[:, :, :-2]) / 6.0
    flat = smoothed.reshape(2, cells, x_count)
    x_cos, x_sin = forward_table(x_count)
    real_part, imag_part = complex_apply("bsx,xq->bqs", flat, None, x_cos, x_sin, 1.0)
    batch = real_part.shape[0]
    y_cos, y_sin = forward_table(y_count)
    z_cos, z_sin = forward_table(z_count)
    zi_cos, zi_sin = inverse_table(z_count)
    yi_cos, yi_sin = inverse_table(y_count)
    xi_cos, xi_sin = inverse_table(x_count)
    real_in = lax.all_to_all(real_part, "py", split_axis=1, concat_axis=2, tiled=True)
    imag_in = lax.all_to_all(imag_part, "py", split_axis=1, concat_axis=2, tiled=True)
    items = real_in.shape[0]

    def relay(values):
        values = values.reshape(items, x_block, y_count, z_local).transpose(0, 2, 1, 3)
        return values.reshape(items, y_count, x_block * z_local)

    real_part, imag_part = complex_apply(
        "byc,yk->bkc", relay(real_in), relay(imag_in), y_cos, y_sin, 1.0
    )
    real_in = lax.all_to_all(real_part, "pz", split_axis=1, concat_axis=2, tiled=True)
    imag_in = lax.all_to_all(imag_part, "pz", split_axis=1, concat_axis=2, tiled=True)
    lines_items = real_in.shape[0]

    def relay(values):
        values = values.reshape(lines_items, ky_block, pz_count, x_block, z_local).transpose(
            0, 1, 3, 2, 4
        )
        return values.reshape(lines_items, ky_block, x_block, z_count)

    real_part, imag_part = complex_apply(
        "bkxz,zm->bkxm", relay(real_in), relay(imag_in), z_cos, z_sin, 1.0
    )
    ky_start = lax.axis_index("pz") * ky_block
    kx_start = lax.axis_index("py") * x_block
    freq_y = freq_at(ky_start + jnp.arange(ky_block, dtype=jnp.int32), y_count)
    freq_x = freq_at(kx_start + jnp.arange(x_block, dtype=jnp.int32), x_count)
    freq_z = freq_at(jnp.arange(z_count, dtype=jnp.int32), z_count)
    kernel = make_kernel(
        coef,
        (freq_y[:, None, None], freq_x[None, :, None], freq_z[None, None, :]),
        (y_count, x_count, z_count),
    )
    real_next = kernel[:, 0] * real_part[0] + kernel[:, 1] * real_part[1]
    imag_next = kernel[:, 0] * imag_part[0] + kernel[:, 1] * imag_part[1]
    real_part = real_next
    imag_part = imag_next
    real_part, imag_part = complex_apply(
        "bkxm,mz->bkxz", real_part, imag_part, zi_cos, zi_sin, -1.0
    )

    def relay_back(values):
        values = values.reshape(batch, ky_block, x_block, pz_count, z_local).transpose(
            0, 1, 3, 2, 4
        )
        return values.reshape(batch, ky_block, pz_count * x_block * z_local)

    real_part = relay_back(real_part)
    imag_part = relay_back(imag_part)
    real_in = lax.all_to_all(real_part, "pz", split_axis=2, concat_axis=1, tiled=True)
    imag_in = lax.all_to_all(imag_part, "pz", split_axis=2, concat_axis=1, tiled=True)
    back_items = real_in.shape[0]
    real_out, imag_out = complex_apply("bkc,ky->byc", real_in, imag_in, yi_cos, yi_sin, -1.0)

    def relay(values):
        values = values.reshape(back_items, y_count, x_block, z_local).transpose(0, 2, 1, 3)
        return values.reshape(back_items, x_block, y_count * z_local)

    real_part = relay(real_out)
    imag_part = relay(imag_out)
    real_in = lax.all_to_all(real_part, "py", split_axis=2, concat_axis=1, tiled=True)
    imag_in = lax.all_to_all(imag_part, "py", split_axis=2, concat_axis=1, tiled=True)
    result = contract("bqs,qx->bsx", real_in, xi_cos) - contract("bqs,qx->bsx", imag_in, xi_sin)
    return (
        result[0].reshape(y_local, z_local, x_count),
        result[1].reshape(y_local, z_local, x_count),
    )


def solution(mesh):
    in_specs = (P("py", "pz", None), P("py", "pz", None), P())
    out_specs = (P("py", "pz", None), P("py", "pz", None))
    return jax.shard_map(shards, mesh=mesh, in_specs=in_specs, out_specs=out_specs, check_vma=False)
```

profile of v0, /device:TPU:0, one launch (start us, length us, event | category | flops | bytes accessed | tf_op | source)
XLA Modules:
  0.0 1785.4 jit_solution(6525902035825200465)
XLA Ops:
  56.9 36.3 %convolution_bitcast_fusion = f32[2,512,2048]{2,1,0:T(8,128)S(1)} fusion(f32[2,2048,512]{2,1,0:T(8,128)} %bitcast.222, s32[512]{0:T(512)S(1)} %fusion.138), kind=kOutput, calls=%fused_computation.64 | convolution fusion | flops 12888571904 | bytes 16779264 | tf_op jit(solution)/shard_map/bsx,xq->bqs/dot_general | solution.py:48
  110.0 48.6 %multiply_bitcast_fusion = f32[2,512,2048]{2,1,0:T(8,128)S(1)} fusion(f32[2,2048,512]{2,1,0:T(8,128)} %bitcast.223, s32[512]{0:T(512)S(1)} %fusion.138), kind=kOutput, calls=%fused_computation.54 | convolution fusion | flops 12890669056 | bytes 16779264 | tf_op jit(solution)/shard_map/bsx,xq->bqs/dot_general | solution.py:48
  169.8 33.0 %all-to-all-done = f32[2,512,2048]{2,0,1:T(2,128)} async-done(((f32[2,512,2048]{2,0,1:T(2,128)}), f32[2,512,2048]{2,0,1:T(2,128)}, u32[]{:S(2)}, u32[]{:S(2)}) %all-to-all-start) | async-done | bytes 8388640 | tf_op jit(solution)/shard_map/all_to_all | solution.py:94
  239.1 62.9 %all-to-all-done.1 = f32[2,512,2048]{2,0,1:T(2,128)} async-done(((f32[2,512,2048]{2,0,1:T(2,128)}), f32[2,512,2048]{2,0,1:T(2,128)}, u32[]{:S(2)}, u32[]{:S(2)}) %all-to-all-start.1) | async-done | bytes 8388640 | tf_op jit(solution)/shard_map/all_to_all | solution.py:95
  406.5 150.7 %all-to-all-done.2 = f32[2,256,4096]{2,0,1:T(2,128)} async-done(((f32[2,256,4096]{2,0,1:T(2,128)}), f32[2,256,4096]{2,0,1:T(2,128)}, u32[]{:S(2)}, u32[]{:S(2)}) %all-to-all-start.2) | async-done | bytes 8388640 | tf_op jit(solution)/shard_map/all_to_all | solution.py:105
  564.1 58.6 %fusion.10 = f32[2,2,32,128,256]{4,1,0,3,2:T(2,128)} fusion(f32[8]{0:T(128)S(1)} %add_multiply_fusion, f32[32,128,256]{2,1,0:T(8,128)S(1)} %sqrt_multiply_fusion, f32[2,2,8]{2,1,0:T(2,128)S(1)} %copy-done), kind=kOutput, calls=%fused_computation.19 | convolution fusion | flops 436207616 | bytes 20971680 | tf_op jit(solution)/shard_map/abr,rkxm->abkxm/dot_general | solution.py:67
  674.5 21.7 %copy.133 = f32[2,32,128,8,32]{2,4,3,1,0:T(8,128)} copy(f32[2,32,128,8,32]{4,2,3,1,0:T(8,128)} %bitcast.202) | data formatting | bytes 16777216 | tf_op jit(solution)/shard_map/transpose | solution.py:110
  715.9 30.5 %all-to-all-done.3 = f32[2,256,4096]{2,0,1:T(2,128)} async-done(((f32[2,256,4096]{2,0,1:T(2,128)}), f32[2,256,4096]{2,0,1:T(2,128)}, u32[]{:S(2)}, u32[]{:S(2)}) %all-to-all-start.3) | async-done | bytes 8388640 | tf_op jit(solution)/shard_map/all_to_all | solution.py:106
  778.0 21.7 %copy.140 = f32[2,32,128,8,32]{2,4,3,1,0:T(8,128)} copy(f32[2,32,128,8,32]{4,2,3,1,0:T(8,128)} %bitcast.203) | data formatting | bytes 16777216 | tf_op jit(solution)/shard_map/transpose | solution.py:110
  866.1 30.2 %fusion.27 = (f32[2,32,128,256]{3,0,2,1:T(2,128)}, f32[2,32,128,256]{3,0,2,1:T(2,128)}) fusion(f32[2,1,32,128,256]{4,1,0,3,2:T(1,128)} %get-tuple-element.5, f32[2,1,32,128,256]{4,1,0,3,2:T(1,128)} %get-tuple-element.4, f32[32,128,256]{2,1,0:T(8,128)} %get-tuple-element.20, f32[32,128,256]{2,1,0:T(8,128)} %get-tuple-element.21, ...), kind=kLoop, calls=%fused_computation.44 | loop fusion | flops 12582912 | bytes 50331648 | tf_op jit(solution)/shard_map/add | solution.py:128
  929.7 28.6 %copy.203 = f32[2,32,8,128,32]{1,0,4,3,2:T(2,128)} copy(f32[2,32,8,128,32]{3,4,2,1,0:T(8,128)} %bitcast.233) | data formatting | bytes 16777216 | tf_op jit(solution)/shard_map/reshape | solution.py:140
  958.3 35.4 %reshape.323 = f32[8,1,262144]{2,1,0:T(1,128)} reshape(f32[32768,2,32]{2,1,0:T(2,128)} %bitcast.204) | data formatting | bytes 16777216
  1034.7 28.6 %copy.208 = f32[2,32,8,128,32]{1,0,4,3,2:T(2,128)} copy(f32[2,32,8,128,32]{3,4,2,1,0:T(8,128)} %bitcast.234) | data formatting | bytes 16777216 | tf_op jit(solution)/shard_map/reshape | solution.py:140
  1063.4 35.8 %reshape.321 = f32[8,1,262144]{2,1,0:T(1,128)} reshape(f32[32768,2,32]{2,1,0:T(2,128)} %bitcast.205) | data formatting | bytes 16777216
  1099.2 83.5 %all-to-all-done.4 = f32[8,1,262144]{2,1,0:T(1,128)} async-done(((f32[8,1,262144]{2,1,0:T(1,128)}), f32[8,1,262144]{2,1,0:T(1,128)}, u32[]{:S(2)}, u32[]{:S(2)}) %all-to-all-start.4) | async-done | bytes 8388640 | tf_op jit(solution)/shard_map/all_to_all | solution.py:144
  1188.2 28.2 %reduce.1 = f32[8,262144]{1,0:T(8,128)} reduce(f32[8,1,262144]{2,1,0:T(1,128)} %all-to-all-done.4, f32[]{:T(128)} %broadcast.767), dimensions={1}, to_apply=%all_to_all.108.reduce_sub_computation | reduce | bytes 16777220 | tf_op jit(solution)/shard_map/all_to_all | solution.py:144
  1216.4 55.1 %reshape.324 = f32[32768,2,32]{2,1,0:T(2,128)} reshape(f32[8,262144]{1,0:T(8,128)} %reduce.1) | data formatting | bytes 16777216
  1271.4 40.0 %copy.205 = f32[2,32,8,4096]{3,1,2,0:T(8,128)} copy(f32[2,32,8,4096]{1,0,3,2:T(2,128)} %bitcast.206) | data formatting | bytes 16777216 | tf_op jit(solution)/shard_map/all_to_all | solution.py:144
  1311.4 60.1 %all-to-all-done.5 = f32[8,1,262144]{2,1,0:T(1,128)} async-done(((f32[8,1,262144]{2,1,0:T(1,128)}), f32[8,1,262144]{2,1,0:T(1,128)}, u32[]{:S(2)}, u32[]{:S(2)}) %all-to-all-start.5) | async-done | bytes 8388640 | tf_op jit(solution)/shard_map/all_to_all | solution.py:145
  1371.5 28.2 %reduce = f32[8,262144]{1,0:T(8,128)} reduce(f32[8,1,262144]{2,1,0:T(1,128)} %all-to-all-done.5, f32[]{:T(128)} %broadcast.767), dimensions={1}, to_apply=%all_to_all.112.reduce_sub_computation | reduce | bytes 16777220 | tf_op jit(solution)/shard_map/all_to_all | solution.py:145
  1399.7 54.9 %reshape.322 = f32[32768,2,32]{2,1,0:T(2,128)} reshape(f32[8,262144]{1,0:T(8,128)} %reduce) | data formatting | bytes 16777216
  1454.6 40.0 %copy.210 = f32[2,32,8,4096]{3,1,2,0:T(8,128)} copy(f32[2,32,8,4096]{1,0,3,2:T(2,128)} %bitcast.207) | data formatting | bytes 16777216 | tf_op jit(solution)/shard_map/all_to_all | solution.py:145
  1623.6 30.8 %all-to-all-done.7 = f32[2,128,8192]{1,0,2:T(2,128)} async-done(((f32[2,128,8192]{1,0,2:T(2,128)}), f32[2,128,8192]{1,0,2:T(2,128)}, u32[]{:S(2)}, u32[]{:S(2)}) %all-to-all-start.7) | async-done | bytes 8388640 | tf_op jit(solution)/shard_map/all_to_all | solution.py:156
  1684.1 67.9 %all-to-all-done.6 = f32[2,128,8192]{1,0,2:T(2,128)} async-done(((f32[2,128,8192]{1,0,2:T(2,128)}), f32[2,128,8192]{1,0,2:T(2,128)}, u32[]{:S(2)}, u32[]{:S(2)}) %all-to-all-start.6) | async-done | bytes 8388640 | tf_op jit(solution)/shard_map/all_to_all | solution.py:155
  (105 shorter events, 672.7 us)
Async XLA Ops:
  0.6 563.5 %copy-start = (f32[2,2,8]{2,1,0:T(2,128)S(1)}, f32[2,2,8]{2,1,0:T(2,128)}, u32[]{:S(2)}) copy-start(f32[2,2,8]{2,1,0:T(2,128)} %param.5) | copy-start | bytes 388
  0.6 13.7 copy-start.5
  0.7 13.6 copy-start.6
  25.9 8.3 collective-permute-start
  29.0 7.5 collective-permute-start.1
  37.0 8.5 collective-permute-start.2
  37.1 8.5 collective-permute-start.3
  40.6 69.3 %copy-start.9 = (s32[512]{0:T(512)}, s32[512]{0:T(512)S(1)}, u32[]{:S(2)}) copy-start(s32[512]{0:T(512)S(1)} %fusion.138) | copy-start | bytes 6148
  104.3 98.5 %all-to-all-start = ((f32[2,512,2048]{2,0,1:T(2,128)}), f32[2,512,2048]{2,0,1:T(2,128)}, u32[]{:S(2)}, u32[]{:S(2)}) async-start(f32[2,512,2048]{2,0,1:T(2,128)} %copy.120), calls=%async_computation | async-start | bytes 16777216 | tf_op jit(solution)/shard_map/all_to_all | solution.py:94
  202.8 99.2 %all-to-all-start.1 = ((f32[2,512,2048]{2,0,1:T(2,128)}), f32[2,512,2048]{2,0,1:T(2,128)}, u32[]{:S(2)}, u32[]{:S(2)}) async-start(f32[2,512,2048]{2,0,1:T(2,128)} %copy.126), calls=%async_computation.1 | async-start | bytes 16777216 | tf_op jit(solution)/shard_map/all_to_all | solution.py:95
  332.7 13.9 copy-start.3
  368.1 189.0 %all-to-all-start.2 = ((f32[2,256,4096]{2,0,1:T(2,128)}), f32[2,256,4096]{2,0,1:T(2,128)}, u32[]{:S(2)}, u32[]{:S(2)}) async-start(f32[2,256,4096]{2,0,1:T(2,128)} %copy.131), calls=%async_computation.2 | async-start | bytes 16777216 | tf_op jit(solution)/shard_map/all_to_all | solution.py:105
  557.1 189.2 %all-to-all-start.3 = ((f32[2,256,4096]{2,0,1:T(2,128)}), f32[2,256,4096]{2,0,1:T(2,128)}, u32[]{:S(2)}, u32[]{:S(2)}) async-start(f32[2,256,4096]{2,0,1:T(2,128)} %copy.138), calls=%async_computation.3 | async-start | bytes 16777216 | tf_op jit(solution)/shard_map/all_to_all | solution.py:106
  799.7 19.4 %copy-start.2 = (f32[2,32,128,8,32]{2,4,3,1,0:T(8,128)S(1)}, f32[2,32,128,8,32]{2,4,3,1,0:T(8,128)}, u32[]{:S(2)}) copy-start(f32[2,32,128,8,32]{2,4,3,1,0:T(8,128)} %copy.140) | copy-start | bytes 25165828
  799.7 40.6 %slice-start = ((s8[8388608]{0:T(1024)(128)(4,1)}), s8[4194304]{0:T(1024)(128)(4,1)S(1)}, s32[]{:S(2)}) async-start(s8[8388608]{0:T(1024)(128)(4,1)} %bitcast.213), calls=%async_computation.8 | async-start | bytes 8388608
  819.1 21.2 %slice-start.1 = ((s8[8388608]{0:T(1024)(128)(4,1)}), s8[4194304]{0:T(1024)(128)(4,1)S(1)}, s32[]{:S(2)}) async-start(s8[8388608]{0:T(1024)(128)(4,1)} %bitcast.213), calls=%async_computation.9 | async-start | bytes 8388608
  840.3 18.4 %copy-start.8 = (f32[2,32,128,256]{3,2,1,0:T(8,128)S(1)}, f32[2,32,128,256]{3,2,1,0:T(8,128)}, u32[]{:S(2)}) copy-start(f32[2,32,128,256]{3,2,1,0:T(8,128)} %convolution_add_fusion) | copy-start | bytes 25165828
  896.4 13.0 copy-start.4
  993.7 189.0 %all-to-all-start.4 = ((f32[8,1,262144]{2,1,0:T(1,128)}), f32[8,1,262144]{2,1,0:T(1,128)}, u32[]{:S(2)}, u32[]{:S(2)}) async-start(f32[8,1,262144]{2,1,0:T(1,128)} %reshape.323), calls=%async_computation.4 | async-start | bytes 16777216 | tf_op jit(solution)/shard_map/all_to_all | solution.py:144
  1182.7 188.8 %all-to-all-start.5 = ((f32[8,1,262144]{2,1,0:T(1,128)}), f32[8,1,262144]{2,1,0:T(1,128)}, u32[]{:S(2)}, u32[]{:S(2)}) async-start(f32[8,1,262144]{2,1,0:T(1,128)} %reshape.321), calls=%async_computation.5 | async-start | bytes 16777216 | tf_op jit(solution)/shard_map/all_to_all | solution.py:145
  1556.3 98.2 %all-to-all-start.7 = ((f32[2,128,8192]{1,0,2:T(2,128)}), f32[2,128,8192]{1,0,2:T(2,128)}, u32[]{:S(2)}, u32[]{:S(2)}) async-start(f32[2,128,8192]{1,0,2:T(2,128)} %copy.172), calls=%async_computation.7 | async-start | bytes 16777216 | tf_op jit(solution)/shard_map/all_to_all | solution.py:156
  1654.4 97.6 %all-to-all-start.6 = ((f32[2,128,8192]{1,0,2:T(2,128)}), f32[2,128,8192]{1,0,2:T(2,128)}, u32[]{:S(2)}, u32[]{:S(2)}) async-start(f32[2,128,8192]{1,0,2:T(2,128)} %copy.167), calls=%async_computation.6 | async-start | bytes 16777216 | tf_op jit(solution)/shard_map/all_to_all | solution.py:155
  1752.0 7.7 copy-start.7
  1759.7 25.5 %copy-start.1 = (f32[2,2,8]{2,1,0:T(2,128)S(1)}, f32[2,2,8]{2,1,0:T(2,128)}, u32[]{:S(2)}) copy-start(f32[2,2,8]{2,1,0:T(2,128)} %param.5) | copy-start | bytes 388
  (1 other events, 3.9 us)
where the time goes:
time: 1800 us; the launch traced here: 1790 us
  local copies, waits for them, and re-layouts  661 us (37%)
  waiting for transfers between devices  531 us (30%)
  matrix products  416 us (23%)
  other arithmetic  125 us (7%)
  starting transfers between devices  51 us (3%)
    dot_general x20, matrix products, contract(): return jnp.einsum(form, data, table, precision=HIGH)  357 us
    unnamed x30, local copies, waits for them, and re-layouts  181 us
    all_to_all x1, waiting for transfers between devices, shards(): lax.all_to_all(real_part, 'pz', split_axis=1, concat_axis=2, tiled=True)  151 us
    all_to_all x1, waiting for transfers between devices, shards(): lax.all_to_all(real_part, 'pz', split_axis=2, concat_axis=1, tiled=True)  83.5 us
    all_to_all x1, waiting for transfers between devices, shards(): lax.all_to_all(real_part, 'py', split_axis=2, concat_axis=1, tiled=True)  67.9 us
    all_to_all x1, waiting for transfers between devices, shards(): lax.all_to_all(imag_part, 'py', split_axis=1, concat_axis=2, tiled=True)  62.9 us
    all_to_all x1, waiting for transfers between devices, shards(): lax.all_to_all(imag_part, 'pz', split_axis=2, concat_axis=1, tiled=True)  60.1 us
    dot_general x1, matrix products, make_kernel(): kernel = jnp.einsum('abr,rkxm->abkxm', coef, basis, precision=HIGH)  58.6 us
  transfers between devices with their start and end apart: 12, of which 11 were waited for; matrix products, arithmetic and copies ran while one was open for 33% of the time, Pallas kernels for 0%

commit v1 on v0

--- a/solution.py
+++ b/solution.py
@@ -141,7 +141,19 @@
 
     real_part = relay_back(real_part)
     imag_part = relay_back(imag_part)
-    real_in = lax.all_to_all(real_part, "pz", split_axis=2, concat_axis=1, tiled=True)
+    ways, here = (lax.axis_size("pz"), lax.axis_index("pz"))
+    width_2 = real_part.shape[2] // ways
+    dims = list(real_part.shape)
+    dims[2] = width_2
+    height = dims[1]
+    dims[1] = height * ways
+    full = jnp.zeros(dims, real_part.dtype)
+    for mask in range(ways):
+        part = lax.dynamic_slice_in_dim(real_part, (here ^ mask) * width_2, width_2, axis=2)
+        if mask:
+            part = lax.ppermute(part, "pz", [(d, d ^ mask) for d in range(ways)])
+        full = lax.dynamic_update_slice_in_dim(full, part, (here ^ mask) * height, axis=1)
+    real_in = full
     imag_in = lax.all_to_all(imag_part, "pz", split_axis=2, concat_axis=1, tiled=True)
     back_items = real_in.shape[0]
     real_out, imag_out = complex_apply("bkc,ky->byc", real_in, imag_in, yi_cos, yi_sin, -1.0)

time: 1800 us -> 1790 us (level)
  the two profiles are of different devices: /device:TPU:0 before, /device:TPU:8 now
where the time goes in v1:
time: 1790 us; the launch traced here: 1780 us
  waiting for transfers between devices  641 us (36%)
  local copies, waits for them, and re-layouts  563 us (31%)
  matrix products  416 us (23%)
  other arithmetic  96.9 us (5%)
  starting transfers between devices  58 us (3%)
    dot_general x20, matrix products, contract(): return jnp.einsum(form, data, table, precision=HIGH)  357 us
    ppermute x7, waiting for transfers between devices, shards(): part = lax.ppermute(part, 'pz', [(d, d ^ mask) for d in range(ways)])  258 us
    all_to_all x1, waiting for transfers between devices, shards(): lax.all_to_all(real_part, 'pz', split_axis=1, concat_axis=2, tiled=True)  147 us
    unnamed x30, local copies, waits for them, and re-layouts  91.5 us
    all_to_all x1, waiting for transfers between devices, shards(): lax.all_to_all(real_part, 'py', split_axis=2, concat_axis=1, tiled=True)  68.3 us
    all_to_all x1, waiting for transfers between devices, shards(): lax.all_to_all(imag_part, 'py', split_axis=1, concat_axis=2, tiled=True)  62.1 us
    dot_general x1, matrix products, make_kernel(): kernel = jnp.einsum('abr,rkxm->abkxm', coef, basis, precision=HIGH)  58.6 us
    reshape x2, local copies, waits for them, and re-layouts, relay_back(): return values.reshape(batch, ky_block, pz_count * x_block * z_local)  49.9 us
  transfers between devices with their start and end apart: 18, of which 16 were waited for; matrix products, arithmetic and copies ran while one was open for 26% of the time, Pallas kernels for 0%

profile of v1, /device:TPU:8, one launch (start us, length us, event | category | flops | bytes accessed | tf_op | source)
XLA Modules:
  0.0 1775.5 jit_solution(15262660960577489617)
XLA Ops:
  55.3 36.3 %convolution_bitcast_fusion = f32[2,512,2048]{2,1,0:T(8,128)S(1)} fusion(f32[2,2048,512]{2,1,0:T(8,128)} %bitcast.212, s32[512]{0:T(512)S(1)} %fusion.158), kind=kOutput, calls=%fused_computation.64 | convolution fusion | flops 12888571904 | bytes 16779264 | tf_op jit(solution)/shard_map/bsx,xq->bqs/dot_general | solution.py:48
  108.4 48.6 %multiply_bitcast_fusion = f32[2,512,2048]{2,1,0:T(8,128)S(1)} fusion(f32[2,2048,512]{2,1,0:T(8,128)} %bitcast.213, s32[512]{0:T(512)S(1)} %fusion.158), kind=kOutput, calls=%fused_computation.54 | convolution fusion | flops 12890669056 | bytes 16779264 | tf_op jit(solution)/shard_map/bsx,xq->bqs/dot_general | solution.py:48
  168.2 33.9 %all-to-all-done = f32[2,512,2048]{2,0,1:T(2,128)} async-done(((f32[2,512,2048]{2,0,1:T(2,128)}), f32[2,512,2048]{2,0,1:T(2,128)}, u32[]{:S(2)}, u32[]{:S(2)}) %all-to-all-start) | async-done | bytes 8388640 | tf_op jit(solution)/shard_map/all_to_all | solution.py:94
  238.3 62.1 %all-to-all-done.1 = f32[2,512,2048]{2,0,1:T(2,128)} async-done(((f32[2,512,2048]{2,0,1:T(2,128)}), f32[2,512,2048]{2,0,1:T(2,128)}, u32[]{:S(2)}, u32[]{:S(2)}) %all-to-all-start.1) | async-done | bytes 8388640 | tf_op jit(solution)/shard_map/all_to_all | solution.py:95
  405.3 147.2 %all-to-all-done.2 = f32[2,256,4096]{2,0,1:T(2,128)} async-done(((f32[2,256,4096]{2,0,1:T(2,128)}), f32[2,256,4096]{2,0,1:T(2,128)}, u32[]{:S(2)}, u32[]{:S(2)}) %all-to-all-start.2) | async-done | bytes 8388640 | tf_op jit(solution)/shard_map/all_to_all | solution.py:105
  562.9 58.6 %fusion.10 = f32[2,2,32,128,256]{4,1,0,3,2:T(2,128)} fusion(f32[8]{0:T(128)S(1)} %add_multiply_fusion, f32[32,128,256]{2,1,0:T(8,128)S(1)} %sqrt_multiply_fusion, f32[2,2,8]{2,1,0:T(2,128)S(1)} %copy-done), kind=kOutput, calls=%fused_computation.19 | convolution fusion | flops 436207616 | bytes 20971680 | tf_op jit(solution)/shard_map/abr,rkxm->abkxm/dot_general | solution.py:67
  673.4 21.7 %copy.130 = f32[2,32,128,8,32]{2,4,3,1,0:T(8,128)} copy(f32[2,32,128,8,32]{4,2,3,1,0:T(8,128)} %bitcast.196) | data formatting | bytes 16777216 | tf_op jit(solution)/shard_map/transpose | solution.py:110
  714.9 26.8 %all-to-all-done.3 = f32[2,256,4096]{2,0,1:T(2,128)} async-done(((f32[2,256,4096]{2,0,1:T(2,128)}), f32[2,256,4096]{2,0,1:T(2,128)}, u32[]{:S(2)}, u32[]{:S(2)}) %all-to-all-start.3) | async-done | bytes 8388640 | tf_op jit(solution)/shard_map/all_to_all | solution.py:106
  773.3 21.7 %copy.137 = f32[2,32,128,8,32]{2,4,3,1,0:T(8,128)} copy(f32[2,32,128,8,32]{4,2,3,1,0:T(8,128)} %bitcast.197) | data formatting | bytes 16777216 | tf_op jit(solution)/shard_map/transpose | solution.py:110
  814.5 21.1 %convolution_add_fusion = f32[2,32,128,256]{3,2,1,0:T(8,128)} fusion(f32[2,32,128,256]{3,2,1,0:T(8,128)} %fusion.91, f32[2,32,128,256]{2,3,1,0:T(8,128)S(1)} %bitcast.207, s32[256]{0:T(256)S(1)} %compare_select_fusion.8), kind=kOutput, calls=%fused_computation.71 | convolution fusion | flops 6445465600 | bytes 25166848 | tf_op jit(solution)/shard_map/bkxz,zm->bkxm/dot_general | solution.py:48
  861.5 30.3 %fusion.27 = (f32[2,32,128,256]{3,0,2,1:T(2,128)}, f32[2,32,128,256]{3,0,2,1:T(2,128)}) fusion(f32[2,1,32,128,256]{4,1,0,3,2:T(1,128)} %get-tuple-element.5, f32[2,1,32,128,256]{4,1,0,3,2:T(1,128)} %get-tuple-element.4, f32[32,128,256]{2,1,0:T(8,128)} %get-tuple-element.28, f32[32,128,256]{2,1,0:T(8,128)} %get-tuple-element.29, ...), kind=kLoop, calls=%fused_computation.44 | loop fusion | flops 12582912 | bytes 50331648 | tf_op jit(solution)/shard_map/add | solution.py:128
  924.6 28.7 %copy.199 = f32[2,32,8,128,32]{1,0,4,3,2:T(2,128)} copy(f32[2,32,8,128,32]{3,4,2,1,0:T(8,128)} %bitcast.223) | data formatting | bytes 16777216 | tf_op jit(solution)/shard_map/reshape | solution.py:140
  953.3 35.4 %reshape.321 = f32[8,1,262144]{2,1,0:T(1,128)} reshape(f32[32768,2,32]{2,1,0:T(2,128)} %bitcast.198) | data formatting | bytes 16777216
  1053.0 21.2 %reshape.296 = f32[2,32,32768]{2,1,0:T(8,128)} reshape(f32[2,32,8,128,32]{4,3,2,1,0:T(8,128)} %copy.149) | data formatting | bytes 16777216 | tf_op jit(solution)/shard_map/reshape | solution.py:140
  1091.7 64.9 %collective-permute-done.5 = f32[2,32,4096]{2,1,0:T(8,128)} collective-permute-done((f32[2,32,4096]{2,1,0:T(8,128)}, f32[2,32,4096]{2,1,0:T(8,128)}, u32[]{:S(2)}, u32[]{:S(2)}) %collective-permute-start.5) | collective-permute-done | bytes 1048608 | tf_op jit(solution)/shard_map/ppermute | solution.py:154
  1180.8 109.3 %collective-permute-done.7 = f32[2,32,4096]{2,1,0:T(8,128)S(1)} collective-permute-done((f32[2,32,4096]{2,1,0:T(8,128)}, f32[2,32,4096]{2,1,0:T(8,128)S(1)}, u32[]{:S(2)}, u32[]{:S(2)}) %collective-permute-start.7) | collective-permute-done | bytes 1048608 | tf_op jit(solution)/shard_map/ppermute | solution.py:154
  1291.2 21.3 %collective-permute-done.8 = f32[2,32,4096]{2,1,0:T(8,128)S(1)} collective-permute-done((f32[2,32,4096]{2,1,0:T(8,128)S(1)}, f32[2,32,4096]{2,1,0:T(8,128)S(1)}, u32[]{:S(2)}, u32[]{:S(2)}) %collective-permute-start.8) | collective-permute-done | bytes 1048608 | tf_op jit(solution)/shard_map/ppermute | solution.py:154
  1313.6 24.0 %collective-permute-done.9 = f32[2,32,4096]{2,1,0:T(8,128)S(1)} collective-permute-done((f32[2,32,4096]{2,1,0:T(8,128)S(1)}, f32[2,32,4096]{2,1,0:T(8,128)S(1)}, u32[]{:S(2)}, u32[]{:S(2)}) %collective-permute-start.9) | collective-permute-done | bytes 1048608 | tf_op jit(solution)/shard_map/ppermute | solution.py:154
  1360.5 28.2 %reduce = f32[8,262144]{1,0:T(8,128)} reduce(f32[8,1,262144]{2,1,0:T(1,128)} %all-to-all-done.4, f32[]{:T(128)} %broadcast.785), dimensions={1}, to_apply=%all_to_all.95.reduce_sub_computation | reduce | bytes 16777220 | tf_op jit(solution)/shard_map/all_to_all | solution.py:157
  1388.6 54.9 %reshape.322 = f32[32768,2,32]{2,1,0:T(2,128)} reshape(f32[8,262144]{1,0:T(8,128)} %reduce) | data formatting | bytes 16777216
  1443.5 40.0 %copy.201 = f32[2,32,8,4096]{3,1,2,0:T(8,128)} copy(f32[2,32,8,4096]{1,0,3,2:T(2,128)} %bitcast.199) | data formatting | bytes 16777216 | tf_op jit(solution)/shard_map/all_to_all | solution.py:157
  1612.5 31.7 %all-to-all-done.6 = f32[2,128,8192]{1,0,2:T(2,128)} async-done(((f32[2,128,8192]{1,0,2:T(2,128)}), f32[2,128,8192]{1,0,2:T(2,128)}, u32[]{:S(2)}, u32[]{:S(2)}) %all-to-all-start.6) | async-done | bytes 8388640 | tf_op jit(solution)/shard_map/all_to_all | solution.py:168
  1673.8 68.3 %all-to-all-done.5 = f32[2,128,8192]{1,0,2:T(2,128)} async-done(((f32[2,128,8192]{1,0,2:T(2,128)}), f32[2,128,8192]{1,0,2:T(2,128)}, u32[]{:S(2)}, u32[]{:S(2)}) %all-to-all-start.5) | async-done | bytes 8388640 | tf_op jit(solution)/shard_map/all_to_all | solution.py:167
  1749.8 21.1 %fusion.37 = f32[2,2048,512]{2,1,0:T(8,128)S(1)} fusion(f32[2,2048,512]{2,1,0:T(8,128)S(1)} %copy-done.8, f32[2,4,256,8,128]{4,3,2,1,0:T(8,128)} %bitcast.220, s32[512]{0:T(512)S(1)} %copy-done.11), kind=kOutput, calls=%fused_computation.69 | convolution fusion | flops 12890931200 | bytes 25167872 | tf_op jit(solution)/shard_map/bqs,qx->bsx/dot_general | solution.py:48
  (125 shorter events, 717.0 us)
Async XLA Ops:
  0.6 562.2 %copy-start = (f32[2,2,8]{2,1,0:T(2,128)S(1)}, f32[2,2,8]{2,1,0:T(2,128)}, u32[]{:S(2)}) copy-start(f32[2,2,8]{2,1,0:T(2,128)} %param.5) | copy-start | bytes 388
  25.8 7.3 collective-permute-start
  27.3 7.5 collective-permute-start.1
  35.4 6.3 collective-permute-start.2
  35.5 8.5 collective-permute-start.3
  37.2 71.2 %copy-start.10 = (s32[512]{0:T(512)}, s32[512]{0:T(512)S(1)}, u32[]{:S(2)}) copy-start(s32[512]{0:T(512)S(1)} %fusion.158) | copy-start | bytes 6148
  102.7 99.3 %all-to-all-start = ((f32[2,512,2048]{2,0,1:T(2,128)}), f32[2,512,2048]{2,0,1:T(2,128)}, u32[]{:S(2)}, u32[]{:S(2)}) async-start(f32[2,512,2048]{2,0,1:T(2,128)} %copy.117), calls=%async_computation | async-start | bytes 16777216 | tf_op jit(solution)/shard_map/all_to_all | solution.py:94
  202.0 98.4 %all-to-all-start.1 = ((f32[2,512,2048]{2,0,1:T(2,128)}), f32[2,512,2048]{2,0,1:T(2,128)}, u32[]{:S(2)}, u32[]{:S(2)}) async-start(f32[2,512,2048]{2,0,1:T(2,128)} %copy.123), calls=%async_computation.1 | async-start | bytes 16777216 | tf_op jit(solution)/shard_map/all_to_all | solution.py:95
  366.6 185.8 %all-to-all-start.2 = ((f32[2,256,4096]{2,0,1:T(2,128)}), f32[2,256,4096]{2,0,1:T(2,128)}, u32[]{:S(2)}, u32[]{:S(2)}) async-start(f32[2,256,4096]{2,0,1:T(2,128)} %copy.128), calls=%async_computation.2 | async-start | bytes 16777216 | tf_op jit(solution)/shard_map/all_to_all | solution.py:105
  552.4 189.2 %all-to-all-start.3 = ((f32[2,256,4096]{2,0,1:T(2,128)}), f32[2,256,4096]{2,0,1:T(2,128)}, u32[]{:S(2)}, u32[]{:S(2)}) async-start(f32[2,256,4096]{2,0,1:T(2,128)} %copy.135), calls=%async_computation.3 | async-start | bytes 16777216 | tf_op jit(solution)/shard_map/all_to_all | solution.py:106
  795.0 19.5 %copy-start.2 = (f32[2,32,128,8,32]{2,4,3,1,0:T(8,128)S(1)}, f32[2,32,128,8,32]{2,4,3,1,0:T(8,128)}, u32[]{:S(2)}) copy-start(f32[2,32,128,8,32]{2,4,3,1,0:T(8,128)} %copy.137) | copy-start | bytes 25165828
  795.0 40.7 %slice-start = ((s8[8388608]{0:T(1024)(128)(4,1)}), s8[4194304]{0:T(1024)(128)(4,1)S(1)}, s32[]{:S(2)}) async-start(s8[8388608]{0:T(1024)(128)(4,1)} %bitcast.201), calls=%async_computation.7 | async-start | bytes 8388608
  814.5 21.1 %slice-start.1 = ((s8[8388608]{0:T(1024)(128)(4,1)}), s8[4194304]{0:T(1024)(128)(4,1)S(1)}, s32[]{:S(2)}) async-start(s8[8388608]{0:T(1024)(128)(4,1)} %bitcast.201), calls=%async_computation.8 | async-start | bytes 8388608
  988.7 371.2 %all-to-all-start.4 = ((f32[8,1,262144]{2,1,0:T(1,128)}), f32[8,1,262144]{2,1,0:T(1,128)}, u32[]{:S(2)}, u32[]{:S(2)}) async-start(f32[8,1,262144]{2,1,0:T(1,128)} %reshape.321), calls=%async_computation.4 | async-start | bytes 16777216 | tf_op jit(solution)/shard_map/all_to_all | solution.py:157
  1083.3 4.6 collective-permute-start.4
  1083.5 73.0 %collective-permute-start.5 = (f32[2,32,4096]{2,1,0:T(8,128)}, f32[2,32,4096]{2,1,0:T(8,128)}, u32[]{:S(2)}, u32[]{:S(2)}) collective-permute-start(f32[2,32,4096]{2,1,0:T(8,128)} %get-tuple-element.15), channel_id=1, source_target_pairs={{0,2},{1,3},{2,0},{3,1},{4,6},{5,7},{6,4},{7,5},{8,10},{9,11},{10,... | collective-permute-start | bytes 3145736 | tf_op jit(solution)/shard_map/ppermute | solution.py:154
  1083.9 94.7 %collective-permute-start.6 = (f32[2,32,4096]{2,1,0:T(8,128)}, f32[2,32,4096]{2,1,0:T(8,128)}, u32[]{:S(2)}, u32[]{:S(2)}) collective-permute-start(f32[2,32,4096]{2,1,0:T(8,128)} %get-tuple-element.14), channel_id=1, source_target_pairs={{0,3},{1,2},{2,1},{3,0},{4,7},{5,6},{6,5},{7,4},{8,11},{9,10},{10,... | collective-permute-start | bytes 3145736 | tf_op jit(solution)/shard_map/ppermute | solution.py:154
  1085.2 204.9 %collective-permute-start.7 = (f32[2,32,4096]{2,1,0:T(8,128)}, f32[2,32,4096]{2,1,0:T(8,128)S(1)}, u32[]{:S(2)}, u32[]{:S(2)}) collective-permute-start(f32[2,32,4096]{2,1,0:T(8,128)} %get-tuple-element.13), channel_id=1, source_target_pairs={{0,4},{1,5},{2,6},{3,7},{4,0},{5,1},{6,2},{7,3},{8,12},{9,13},{10,... | collective-permute-start | bytes 3145736 | tf_op jit(solution)/shard_map/ppermute | solution.py:154
  1087.7 224.9 %collective-permute-start.8 = (f32[2,32,4096]{2,1,0:T(8,128)S(1)}, f32[2,32,4096]{2,1,0:T(8,128)S(1)}, u32[]{:S(2)}, u32[]{:S(2)}) collective-permute-start(f32[2,32,4096]{2,1,0:T(8,128)S(1)} %get-tuple-element.12), channel_id=1, source_target_pairs={{0,5},{1,4},{2,7},{3,6},{4,1},{5,0},{6,3},{7,2},{8,13},{9,12},{10,... | collective-permute-start | bytes 3145736 | tf_op jit(solution)/shard_map/ppermute | solution.py:154
  1087.9 249.6 %collective-permute-start.9 = (f32[2,32,4096]{2,1,0:T(8,128)S(1)}, f32[2,32,4096]{2,1,0:T(8,128)S(1)}, u32[]{:S(2)}, u32[]{:S(2)}) collective-permute-start(f32[2,32,4096]{2,1,0:T(8,128)S(1)} %get-tuple-element.11), channel_id=1, source_target_pairs={{0,6},{1,7},{2,4},{3,5},{4,2},{5,3},{6,0},{7,1},{8,14},{9,15},{10,... | collective-permute-start | bytes 3145736 | tf_op jit(solution)/shard_map/ppermute | solution.py:154
  1156.6 202.3 %collective-permute-start.10 = (f32[2,32,4096]{2,1,0:T(8,128)S(1)}, f32[2,32,4096]{2,1,0:T(8,128)S(1)}, u32[]{:S(2)}, u32[]{:S(2)}) collective-permute-start(f32[2,32,4096]{2,1,0:T(8,128)S(1)} %get-tuple-element.10), channel_id=1, source_target_pairs={{0,7},{1,6},{2,5},{3,4},{4,3},{5,2},{6,1},{7,0},{8,15},{9,14},{10,... | collective-permute-start | bytes 3145736 | tf_op jit(solution)/shard_map/ppermute | solution.py:154
  1545.2 99.0 %all-to-all-start.6 = ((f32[2,128,8192]{1,0,2:T(2,128)}), f32[2,128,8192]{1,0,2:T(2,128)}, u32[]{:S(2)}, u32[]{:S(2)}) async-start(f32[2,128,8192]{1,0,2:T(2,128)} %copy.166), calls=%async_computation.6 | async-start | bytes 16777216 | tf_op jit(solution)/shard_map/all_to_all | solution.py:168
  1644.2 97.9 %all-to-all-start.5 = ((f32[2,128,8192]{1,0,2:T(2,128)}), f32[2,128,8192]{1,0,2:T(2,128)}, u32[]{:S(2)}, u32[]{:S(2)}) async-start(f32[2,128,8192]{1,0,2:T(2,128)} %copy.161), calls=%async_computation.5 | async-start | bytes 16777216 | tf_op jit(solution)/shard_map/all_to_all | solution.py:167
  1749.8 25.5 %copy-start.1 = (f32[2,2,8]{2,1,0:T(2,128)S(1)}, f32[2,2,8]{2,1,0:T(2,128)}, u32[]{:S(2)}) copy-start(f32[2,2,8]{2,1,0:T(2,128)} %param.5) | copy-start | bytes 388
  (8 other events, 90.5 us)
